TPU v7x, 256 devices: a whole 4x4x8 slice. The times are simulated.
256 devices in a mesh: comp: 16 (over z, core), blk: 16 (over x, y).
Axes of the slice: x: 4, y: 4, z: 8, core: 2. Of those that a mesh axis runs over, the one named last changes fastest.
Arguments:
- state_now: float32 [16, 6, 128, 32, 256], P('comp', None, 'blk'), may hold values from -5 to 5
- state_prev: float32 [16, 6, 128, 32, 256], P('comp', None, 'blk'), may hold values from -5 to 5
- viscosity: float32 [16, 128, 32, 256], P('comp', 'blk'), may hold values from 0.05 to 0.5
- jacobian: float32 [16, 3, 6, 6], P('comp'), may hold values from -0.4 to 0.4
- donor_cell: int32 [16, 16, 16, 2, 8, 128], P('comp', 'blk'), may hold values from 0 to 57343, as said below
- interp_weight: float32 [16, 16, 16, 2, 8, 128], P('comp', 'blk'), may hold values from 0 to 1
- recv_cell: int32 [16, 16, 16, 2, 128], P('comp', 'blk'), may hold values from 0 to 57343, as said below
- pair_tiles: int32 [16, 16, 16], P('blk'), may hold values from 0 to 2, as said below
Outputs:
- state_next: float32 [16, 6, 128, 32, 256], P('comp', None, 'blk')
Inputs may be any that keep to these rules, and one draw needn't show every extreme that they name: `donor_cell`: the cells of one donor tile point are the eight corners of a cube of adjacent cells, corner k = 4 i + 2 j + l offset by (i, j, l). `recv_cell`: the receiving cells of one device are all different. `pair_tiles`: for each block index some destination component takes 2 tiles from every source component.
All inputs are finite; a program needn't handle non-finite values.
Results may differ from a plain program's by a relative error of at most 0.0003.
Values sent between devices are 32-bit elements; how exact they have to be, the bound alone decides.
No kernel may reach another device: no remote copies, remote signals or barrier semaphores. Data moves between devices by JAX's collectives and lax.ppermute only.
A program may use at most 128 MiB of HBM per device.

v0:
```python
import jax
import jax.numpy as jnp
from jax import lax
from jax.sharding import PartitionSpec as P

SUBITERS = 2
time_scale = 0.5
pseudo_diag = 2.5


def padded_2(block, sides, width):
    for axis, dim in sides:
        count = lax.axis_size(axis)
        forward = [(i, i + 1) for i in range(count - 1)]
        backward = [(target, source) for source, target in forward]
        low = lax.ppermute(
            lax.slice_in_dim(block, block.shape[dim] - width, None, axis=dim), axis, forward
        )
        high = lax.ppermute(lax.slice_in_dim(block, 0, width, axis=dim), axis, backward)
        block = jnp.concatenate([low, block, high], axis=dim)
    return block


def mix(jac_dim, field):
    return jnp.einsum("vw,wxyz->vxyz", jac_dim, field, precision=lax.Precision.HIGHEST)


def flux(padded, kappa, jac):
    centre = padded[:, 1:-1]
    along_x = (padded[:, 2:] - padded[:, :-2]) * 0.5
    spread = jnp.pad(centre, ((0, 0), (0, 0), (1, 1), (1, 1)))
    along_y = (spread[:, :, 2:, 1:-1] - spread[:, :, :-2, 1:-1]) * 0.5
    along_z = (spread[:, :, 1:-1, 2:] - spread[:, :, 1:-1, :-2]) * 0.5
    beside = padded[:, 2:] + padded[:, :-2] + spread[:, :, 2:, 1:-1] + spread[:, :, :-2, 1:-1]
    beside = beside + spread[:, :, 1:-1, 2:] + spread[:, :, 1:-1, :-2]
    convect = mix(jac[0], along_x) + mix(jac[1], along_y) + mix(jac[2], along_z)
    return convect + kappa * (6.0 * centre - beside)


def relax(rstar, padded_step, kappa, diag, jac):
    centre = padded_step[:, 1:-1]
    return -(rstar + flux(padded_step, kappa, jac) - 6.0 * kappa * centre) / diag


def shards(
    state_now, state_prev, viscosity, jacobian, donor_cell, interp_weight, recv_cell, pair_tiles
):
    now = state_now[0]
    prev = state_prev[0]
    kappa = viscosity[0]
    jac = jacobian[0]
    nvar, rows, width_y, width_z = now.shape
    total_cells = rows * width_y * width_z
    comps = lax.axis_size("comp")
    mine = lax.axis_index("comp")
    slots = donor_cell.shape[3]
    tile = donor_cell.shape[5]
    diag = pseudo_diag + 6.0 * kappa
    live = lax.dynamic_index_in_dim(pair_tiles[0], mine, 1, keepdims=False)
    keep = jnp.arange(slots, dtype=jnp.int32)[None, :] < live[:, None]
    keep = jnp.broadcast_to(keep[:, :, None], (comps, slots, tile)).reshape(-1)
    cells = recv_cell[0, 0].reshape(-1)
    target_cell = jnp.where(keep, cells, total_cells)
    corner_cell = donor_cell[0, 0].reshape(-1)
    weights = interp_weight[0, 0]
    held = lax.all_to_all(weights, "comp", split_axis=0, concat_axis=0, tiled=True)
    state = now
    for sub in range(SUBITERS):
        padded = padded_2(state, (("blk", 1),), 1)
        rstar = time_scale * (3.0 * state - 4.0 * now + prev) + flux(padded, kappa, jac)
        step = -rstar / diag
        for sweep in range(2):
            padded_step = padded_2(step, (("blk", 1),), 1)
            step = relax(rstar, padded_step, kappa, diag, jac)
        state = state + step
        flat = state.reshape(nvar, total_cells)
        values = flat[:, corner_cell].reshape(nvar, comps, slots, 8, tile)
        packed = jnp.einsum("vcskp,cskp->vcsp", values, held, precision=lax.Precision.HIGHEST)
        arrived = lax.all_to_all(packed, "comp", split_axis=1, concat_axis=1, tiled=True)
        incoming = arrived.reshape(nvar, -1)
        flat = flat.at[:, target_cell].set(incoming, mode="drop")
        state = flat.reshape(nvar, rows, width_y, width_z)
    return state[None]


def solution(mesh):
    in_specs = (
        P("comp", None, "blk", None, None),
        P("comp", None, "blk", None, None),
        P("comp", "blk", None, None),
        P("comp", None, None, None),
        P("comp", "blk", None, None, None, None),
        P("comp", "blk", None, None, None, None),
        P("comp", "blk", None, None, None),
        P("blk", None, None),
    )
    out_specs = P("comp", None, "blk", None, None)
    return jax.shard_map(shards, mesh=mesh, in_specs=in_specs, out_specs=out_specs, check_vma=False)
```

profile of v0, /device:TPU:27, one launch (start us, length us, event | category | flops | bytes accessed | tf_op | source)
XLA Modules:
  0.0 560.0 jit_solution(3538027819280823225)
XLA Ops:
  0.0 9.3 %all-to-all-start = ((f32[16,2,8,128]{3,2,1,0:T(8,128)}), f32[16,2,8,128]{3,2,1,0:T(8,128)S(1)}, u32[]{:S(2)}, u32[]{:S(2)}) async-start(f32[16,2,8,128]{3,2,1,0:T(8,128)} %bitcast.167), calls=%async_computation | async-start | bytes 262144 | tf_op jit(solution)/shard_map/all_to_all | solution.py:66
  9.3 2.4 copy.148
  12.4 2.8 collective-permute-start.1
  15.2 2.5 collective-permute-start
  18.3 2.6 fusion.73
  21.0 2.0 fusion.76
  23.1 3.7 collective-permute-done
  26.8 7.2 %negate_divide_fusion.1 = (f32[6,8,32,256]{3,0,2,1:T(8,128)S(1)}, f32[6,8,32,256]{3,0,2,1:T(8,128)S(1)}) fusion(f32[8,32,256]{2,1,0:T(8,128)S(1)} %get-tuple-element.18, f32[6,8,32,256]{3,0,2,1:T(8,128)S(1)} %bitcast.147, f32[6,1,32,256]{3,0,2,1:T(8,128)} %collective-permute-done.1, f32[6,1,32,256]{3,0,2,1:T(8,128)} %collective-permute-done, ...), kind=kOutput, calls=%fused_computation.119 | convolution fusion | flops 38141952 | bytes 14683136 | tf_op jit(solution)/shard_map/vw,wxyz->vxyz/dot_general | solution.py:25
  34.1 2.6 fusion.64
  38.6 3.6 collective-permute-start.2
  42.2 2.0 fusion.67
  45.2 4.0 collective-permute-done.2
  49.2 3.9 fusion.18
  53.2 2.6 fusion.53
  57.7 3.9 collective-permute-start.4
  61.6 2.0 fusion.56
  63.7 3.9 collective-permute-done.4
  67.6 4.9 fusion.14
  72.5 16.8 %copy.60 = f32[6,65536]{0,1:T(8,128)} copy(f32[6,65536]{1,0:T(8,128)S(1)} %bitcast.151) | data formatting | bytes 3145728 | tf_op jit(solution)/shard_map/reshape | solution.py:76
  89.3 118.8 %gather_fusion = f32[32768,6]{1,0:T(8,128)} fusion(f32[6,65536]{0,1:T(8,128)} %copy.60, s32[32768]{0:T(1024)S(1)} %broadcast_clamp_fusion), kind=kCustom, calls=%fused_computation | custom fusion | bytes 1703936 | tf_op jit(solution)/shard_map/gather | solution.py:77
  208.1 7.7 %multiply_reduce_fusion.1 = f32[16,2,128,6]{3,2,1,0:T(8,128)S(1)} fusion(f32[16,2,128,8,6]{4,2,3,1,0:T(8,128)} %bitcast.148, f32[16,2,128,8]{2,3,1,0:T(8,128)S(1)} %bitcast.152), kind=kLoop, calls=%fused_computation.5 | loop fusion | flops 368640 | bytes 1015808
  217.1 9.3 %all-to-all-start.1 = ((f32[6,16,2,128]{3,2,0,1:T(2,128)}), f32[6,16,2,128]{3,2,0,1:T(2,128)S(1)}, u32[]{:S(2)}, u32[]{:S(2)}) async-start(f32[6,16,2,128]{3,2,0,1:T(2,128)} %bitcast.37), calls=%async_computation.1 | async-start | bytes 196608 | tf_op jit(solution)/shard_map/all_to_all | solution.py:79
  226.5 8.4 %all-to-all-done.1 = f32[6,16,2,128]{3,2,0,1:T(2,128)S(1)} async-done(((f32[6,16,2,128]{3,2,0,1:T(2,128)}), f32[6,16,2,128]{3,2,0,1:T(2,128)S(1)}, u32[]{:S(2)}, u32[]{:S(2)}) %all-to-all-start.1) | async-done | bytes 98336 | tf_op jit(solution)/shard_map/all_to_all | solution.py:79
  235.7 32.3 %scatter_fusion = f32[6,65536]{0,1:T(8,128)} fusion(f32[6,65536]{0,1:T(8,128)} %copy.60, s32[4096]{0:T(1024)S(1)} %bitcast.164, f32[4096,6]{1,0:T(8,128)S(1)} %copy.61), kind=kCustom, calls=%fused_computation.2 | custom fusion | bytes 311296 | tf_op jit(solution)/shard_map/scatter | solution.py:81
  268.0 17.8 %copy.70 = f32[6,8,32,256]{3,0,2,1:T(8,128)S(1)} copy(f32[6,8,32,256]{0,3,2,1:T(8,128)} %bitcast.142) | data formatting | bytes 3145728 | tf_op jit(solution)/shard_map/reshape | solution.py:82
  285.8 2.6 fusion.42
  288.5 1.9 collective-permute-start.7
  290.5 3.6 collective-permute-start.6
  294.1 2.1 fusion.45
  296.2 2.3 collective-permute-done.7
  298.4 4.3 collective-permute-done.6
  302.8 5.8 %negate_divide_fusion = (f32[6,8,32,256]{3,0,2,1:T(8,128)S(1)}, f32[6,8,32,256]{3,0,2,1:T(8,128)S(1)}) fusion(f32[8,32,256]{2,1,0:T(8,128)S(1)} %get-tuple-element.18, f32[6,8,32,256]{3,0,2,1:T(8,128)S(1)} %copy.70, f32[6,1,32,256]{3,0,2,1:T(8,128)S(1)} %collective-permute-done.7, f32[6,1,32,256]{3,0,2,1:T(8,128)S(1)} %collective-permute-done.6, ...), kind=kOutput, calls=%fused_computation.91 | convolution fusion | flops 38141952 | bytes 16256000 | tf_op jit(solution)/shard_map/vw,wxyz->vxyz/dot_general | solution.py:25
  308.6 2.6 fusion.33
  313.1 3.6 collective-permute-start.8
  316.7 2.1 fusion.36
  320.3 4.0 collective-permute-done.8
  324.3 4.2 fusion.8
  328.6 2.6 fusion.22
  333.2 3.6 collective-permute-start.10
  336.8 2.1 fusion.25
  339.3 4.0 collective-permute-done.10
  343.4 5.8 %fusion.4 = f32[6,8,32,256]{3,0,2,1:T(8,128)} fusion(f32[6,8,32,256]{3,0,2,1:T(8,128)S(1)} %copy.70, f32[6,8,32,256]{3,0,2,1:T(8,128)S(1)} %get-tuple-element.25, f32[6,8,32,256]{3,0,2,1:T(8,128)S(1)} %fusion.8, f32[8,32,256,6]{2,3,1,0:T(8,128)S(1)} %fusion.22, f32[8,32,256,6]{2,3,1,0:T(8,128)S(1)} %fusion.25, ...), kind=kOutput, calls=%fused_computation.47 | convolution fusion | flops 37355520 | bytes 15993856 | tf_op jit(solution)/shard_map/vw,wxyz->vxyz/dot_general | solution.py:25
  349.2 16.4 %copy.73 = f32[6,65536]{0,1:T(8,128)} copy(f32[6,65536]{1,0:T(8,128)} %bitcast.150) | data formatting | bytes 3145728 | tf_op jit(solution)/shard_map/reshape | solution.py:76
  365.6 118.8 %gather_fusion.1 = f32[32768,6]{1,0:T(8,128)} fusion(f32[6,65536]{0,1:T(8,128)} %copy.73, s32[32768]{0:T(1024)S(1)} %broadcast_clamp_fusion), kind=kCustom, calls=%fused_computation.1 | custom fusion | bytes 1703936 | tf_op jit(solution)/shard_map/gather | solution.py:77
  484.4 7.7 %multiply_reduce_fusion = f32[16,2,128,6]{3,2,1,0:T(8,128)S(1)} fusion(f32[16,2,128,8,6]{4,2,3,1,0:T(8,128)} %bitcast.149, f32[16,2,128,8]{2,3,1,0:T(8,128)S(1)} %bitcast.153), kind=kLoop, calls=%fused_computation.4 | loop fusion | flops 368640 | bytes 1015808
  492.7 13.4 %all_to_all.15 = f32[6,16,2,128]{3,2,0,1:T(2,128)S(1)} all-to-all(f32[6,16,2,128]{3,2,0,1:T(2,128)S(1)} %bitcast.157), channel_id=1, replica_groups=mesh['comp'=16,'blk'=16] {'comp'}, dimensions={1} | all-to-all | bytes 196608 | tf_op jit(solution)/shard_map/all_to_all | solution.py:79
  506.9 32.2 %scatter_fusion.1 = f32[6,65536]{0,1:T(8,128)} fusion(f32[6,65536]{0,1:T(8,128)} %copy.73, s32[4096]{0:T(1024)S(1)} %bitcast.165, f32[4096,6]{1,0:T(8,128)S(1)} %copy.74), kind=kCustom, calls=%fused_computation.3 | custom fusion | bytes 311296 | tf_op jit(solution)/shard_map/scatter | solution.py:81
  539.1 20.5 %copy.75 = f32[1,6,8,32,256]{4,3,2,1,0:T(8,128)} copy(f32[1,6,8,32,256]{1,4,3,2,0:T(8,128)} %bitcast.143) | data formatting | bytes 3145728 | tf_op jit(solution)/shard_map/broadcast_in_dim;reshape | solution.py:83
  (53 shorter events, 15.5 us)
Async XLA Ops:
  0.0 17.7 %copy-start = (s32[1,16,16]{2,1,0:T(8,128)S(1)}, s32[1,16,16]{2,1,0:T(8,128)}, u32[]{:S(2)}) copy-start(s32[1,16,16]{2,1,0:T(8,128)} %param.15) | copy-start | bytes 3076
  0.0 208.1 %all-to-all-start = ((f32[16,2,8,128]{3,2,1,0:T(8,128)}), f32[16,2,8,128]{3,2,1,0:T(8,128)S(1)}, u32[]{:S(2)}, u32[]{:S(2)}) async-start(f32[16,2,8,128]{3,2,1,0:T(8,128)} %bitcast.167), calls=%async_computation | async-start | bytes 262144 | tf_op jit(solution)/shard_map/all_to_all | solution.py:66
  9.3 8.8 %copy-start.7 = (f32[1,3,6,6]{3,0,2,1:T(1,128)S(1)}, f32[1,3,6,6]{3,0,2,1:T(1,128)}, u32[]{:S(2)}) copy-start(f32[1,3,6,6]{3,0,2,1:T(1,128)} %param.11) | copy-start | bytes 1300
  9.3 8.8 %copy-start.5 = (s32[1,1,16,2,8,128]{5,4,3,2,1,0:T(8,128)S(1)}, s32[1,1,16,2,8,128]{5,4,3,2,1,0:T(8,128)}, u32[]{:S(2)}) copy-start(s32[1,1,16,2,8,128]{5,4,3,2,1,0:T(8,128)} %param.12) | copy-start | bytes 393220
  12.4 10.7 %collective-permute-start.1 = (f32[6,1,32,256]{3,0,2,1:T(8,128)}, f32[6,1,32,256]{3,0,2,1:T(8,128)}, u32[]{:S(2)}, u32[]{:S(2)}) collective-permute-start(f32[6,1,32,256]{3,0,2,1:T(8,128)} %get-tuple-element.15), channel_id=1, source_target_pairs={{0,1},{1,2},{2,3},{3,4},{4,5},{5,6},{6,7},{7,8},{8,9},{9,10},{10,1... | collective-permute-start | bytes 589832 | tf_op jit(solution)/shard_map/ppermute | solution.py:16
  15.2 11.6 %collective-permute-start = (f32[6,1,32,256]{3,0,2,1:T(8,128)S(1)}, f32[6,1,32,256]{3,0,2,1:T(8,128)}, u32[]{:S(2)}, u32[]{:S(2)}) collective-permute-start(f32[6,1,32,256]{3,0,2,1:T(8,128)S(1)} %get-tuple-element.16), channel_id=1, source_target_pairs={{1,0},{2,1},{3,2},{4,3},{5,4},{6,5},{7,6},{8,7},{9,8},{10,9},{11,1... | collective-permute-start | bytes 589832 | tf_op jit(solution)/shard_map/ppermute | solution.py:19
  21.0 2.1 copy-start.4
  21.0 5.9 %copy-start.8 = (f32[1,6,8,32,256]{4,3,2,1,0:T(8,128)S(1)}, f32[1,6,8,32,256]{4,3,2,1,0:T(8,128)}, u32[]{:S(2)}) copy-start(f32[1,6,8,32,256]{4,3,2,1,0:T(8,128)} %param.9) | copy-start | bytes 4718596
  36.7 8.5 %collective-permute-start.3 = (f32[6,1,32,256]{3,0,2,1:T(8,128)S(1)}, f32[6,1,32,256]{3,0,2,1:T(8,128)S(1)}, u32[]{:S(2)}, u32[]{:S(2)}) collective-permute-start(f32[6,1,32,256]{3,0,2,1:T(8,128)S(1)} %get-tuple-element.13), channel_id=1, source_target_pairs={{0,1},{1,2},{2,3},{3,4},{4,5},{5,6},{6,7},{7,8},{8,9},{9,10},{10,1... | collective-permute-start | bytes 589832 | tf_op jit(solution)/shard_map/ppermute | solution.py:16
  38.6 10.6 %collective-permute-start.2 = (f32[6,1,32,256]{3,0,2,1:T(8,128)S(1)}, f32[6,1,32,256]{3,0,2,1:T(8,128)S(1)}, u32[]{:S(2)}, u32[]{:S(2)}) collective-permute-start(f32[6,1,32,256]{3,0,2,1:T(8,128)S(1)} %get-tuple-element.14), channel_id=1, source_target_pairs={{1,0},{2,1},{3,2},{4,3},{5,4},{6,5},{7,6},{8,7},{9,8},{10,9},{11,1... | collective-permute-start | bytes 589832 | tf_op jit(solution)/shard_map/ppermute | solution.py:19
  55.8 7.9 %collective-permute-start.5 = (f32[6,1,32,256]{3,0,2,1:T(8,128)S(1)}, f32[6,1,32,256]{3,0,2,1:T(8,128)S(1)}, u32[]{:S(2)}, u32[]{:S(2)}) collective-permute-start(f32[6,1,32,256]{3,0,2,1:T(8,128)S(1)} %get-tuple-element.11), channel_id=1, source_target_pairs={{0,1},{1,2},{2,3},{3,4},{4,5},{5,6},{6,7},{7,8},{8,9},{9,10},{10,1... | collective-permute-start | bytes 589832 | tf_op jit(solution)/shard_map/ppermute | solution.py:16
  57.7 9.8 %copy-start.2 = (f32[1,6,8,32,256]{4,3,2,1,0:T(8,128)S(1)}, f32[1,6,8,32,256]{4,3,2,1,0:T(8,128)}, u32[]{:S(2)}) copy-start(f32[1,6,8,32,256]{4,3,2,1,0:T(8,128)} %param.8) | copy-start | bytes 4718596
  57.7 9.8 %collective-permute-start.4 = (f32[6,1,32,256]{3,0,2,1:T(8,128)S(1)}, f32[6,1,32,256]{3,0,2,1:T(8,128)S(1)}, u32[]{:S(2)}, u32[]{:S(2)}) collective-permute-start(f32[6,1,32,256]{3,0,2,1:T(8,128)S(1)} %get-tuple-element.12), channel_id=1, source_target_pairs={{1,0},{2,1},{3,2},{4,3},{5,4},{6,5},{7,6},{8,7},{9,8},{10,9},{11,1... | collective-permute-start | bytes 589832 | tf_op jit(solution)/shard_map/ppermute | solution.py:19
  215.8 10.6 %copy-start.6 = (s32[1,1,16,2,128]{4,3,2,1,0:T(2,128)S(1)}, s32[1,1,16,2,128]{4,3,2,1,0:T(2,128)}, u32[]{:S(2)}) copy-start(s32[1,1,16,2,128]{4,3,2,1,0:T(2,128)} %param.14) | copy-start | bytes 49156
  217.1 17.8 %all-to-all-start.1 = ((f32[6,16,2,128]{3,2,0,1:T(2,128)}), f32[6,16,2,128]{3,2,0,1:T(2,128)S(1)}, u32[]{:S(2)}, u32[]{:S(2)}) async-start(f32[6,16,2,128]{3,2,0,1:T(2,128)} %bitcast.37), calls=%async_computation.1 | async-start | bytes 196608 | tf_op jit(solution)/shard_map/all_to_all | solution.py:79
  288.5 9.9 %collective-permute-start.7 = (f32[6,1,32,256]{3,0,2,1:T(8,128)S(1)}, f32[6,1,32,256]{3,0,2,1:T(8,128)S(1)}, u32[]{:S(2)}, u32[]{:S(2)}) collective-permute-start(f32[6,1,32,256]{3,0,2,1:T(8,128)S(1)} %get-tuple-element.9), channel_id=1, source_target_pairs={{0,1},{1,2},{2,3},{3,4},{4,5},{5,6},{6,7},{7,8},{8,9},{9,10},{10,1... | collective-permute-start | bytes 589832 | tf_op jit(solution)/shard_map/ppermute | solution.py:16
  290.4 12.3 %copy-start.3 = (f32[1,6,8,32,256]{4,3,2,1,0:T(8,128)S(1)}, f32[1,6,8,32,256]{4,3,2,1,0:T(8,128)}, u32[]{:S(2)}) copy-start(f32[1,6,8,32,256]{4,3,2,1,0:T(8,128)} %param.8) | copy-start | bytes 4718596
  290.4 12.3 %copy-start.9 = (f32[1,6,8,32,256]{4,3,2,1,0:T(8,128)S(1)}, f32[1,6,8,32,256]{4,3,2,1,0:T(8,128)}, u32[]{:S(2)}) copy-start(f32[1,6,8,32,256]{4,3,2,1,0:T(8,128)} %param.9) | copy-start | bytes 4718596
  290.5 12.3 %collective-permute-start.6 = (f32[6,1,32,256]{3,0,2,1:T(8,128)S(1)}, f32[6,1,32,256]{3,0,2,1:T(8,128)S(1)}, u32[]{:S(2)}, u32[]{:S(2)}) collective-permute-start(f32[6,1,32,256]{3,0,2,1:T(8,128)S(1)} %get-tuple-element.10), channel_id=1, source_target_pairs={{1,0},{2,1},{3,2},{4,3},{5,4},{6,5},{7,6},{8,7},{9,8},{10,9},{11,1... | collective-permute-start | bytes 589832 | tf_op jit(solution)/shard_map/ppermute | solution.py:19
  311.2 9.0 %collective-permute-start.9 = (f32[6,1,32,256]{3,0,2,1:T(8,128)S(1)}, f32[6,1,32,256]{3,0,2,1:T(8,128)S(1)}, u32[]{:S(2)}, u32[]{:S(2)}) collective-permute-start(f32[6,1,32,256]{3,0,2,1:T(8,128)S(1)} %get-tuple-element.7), channel_id=1, source_target_pairs={{0,1},{1,2},{2,3},{3,4},{4,5},{5,6},{6,7},{7,8},{8,9},{9,10},{10,1... | collective-permute-start | bytes 589832 | tf_op jit(solution)/shard_map/ppermute | solution.py:16
  313.1 11.2 %collective-permute-start.8 = (f32[6,1,32,256]{3,0,2,1:T(8,128)S(1)}, f32[6,1,32,256]{3,0,2,1:T(8,128)S(1)}, u32[]{:S(2)}, u32[]{:S(2)}) collective-permute-start(f32[6,1,32,256]{3,0,2,1:T(8,128)S(1)} %get-tuple-element.8), channel_id=1, source_target_pairs={{1,0},{2,1},{3,2},{4,3},{5,4},{6,5},{7,6},{8,7},{9,8},{10,9},{11,1... | collective-permute-start | bytes 589832 | tf_op jit(solution)/shard_map/ppermute | solution.py:19
  331.2 8.1 %collective-permute-start.11 = (f32[6,1,32,256]{3,0,2,1:T(8,128)S(1)}, f32[6,1,32,256]{3,0,2,1:T(8,128)S(1)}, u32[]{:S(2)}, u32[]{:S(2)}) collective-permute-start(f32[6,1,32,256]{3,0,2,1:T(8,128)S(1)} %get-tuple-element.5), channel_id=1, source_target_pairs={{0,1},{1,2},{2,3},{3,4},{4,5},{5,6},{6,7},{7,8},{8,9},{9,10},{10,1... | collective-permute-start | bytes 589832 | tf_op jit(solution)/shard_map/ppermute | solution.py:16
  333.2 10.2 %collective-permute-start.10 = (f32[6,1,32,256]{3,0,2,1:T(8,128)S(1)}, f32[6,1,32,256]{3,0,2,1:T(8,128)S(1)}, u32[]{:S(2)}, u32[]{:S(2)}) collective-permute-start(f32[6,1,32,256]{3,0,2,1:T(8,128)S(1)} %get-tuple-element.6), channel_id=1, source_target_pairs={{1,0},{2,1},{3,2},{4,3},{5,4},{6,5},{7,6},{8,7},{9,8},{10,9},{11,1... | collective-permute-start | bytes 589832 | tf_op jit(solution)/shard_map/ppermute | solution.py:19
  539.1 20.5 %copy-start.1 = (s32[1,16,16]{2,1,0:T(8,128)S(1)}, s32[1,16,16]{2,1,0:T(8,128)}, u32[]{:S(2)}) copy-start(s32[1,16,16]{2,1,0:T(8,128)} %param.15) | copy-start | bytes 3076
where the time goes:
time: 570 us; the launch traced here: 560 us
  local copies, waits for them, and re-layouts  381 us (67%)
  matrix products  59.9 us (11%)
  starting transfers between devices  51.8 us (9%)
  waiting for transfers between devices  37.6 us (7%)
  other arithmetic  15.7 us (3%)
  blocking collectives  13.4 us (2%)
    gather x2, local copies, waits for them, and re-layouts, shards(): values = flat[:, corner_cell].reshape(nvar, comps, slots, 8, tile)  238 us
    scatter x2, local copies, waits for them, and re-layouts, shards(): flat = flat.at[:, target_cell].set(incoming, mode='drop')  64.5 us
    dot_general x18, matrix products, mix(): jnp.einsum('vw,wxyz->vxyz', jac_dim, field, precision=lax.Precision.HIGHEST)  59.9 us
    reshape x2, local copies, waits for them, and re-layouts, shards(): flat = state.reshape(nvar, total_cells)  33.2 us
    ppermute x6, waiting for transfers between devices, padded_2(): lax.ppermute(lax.slice_in_dim(block, 0, width, axis=dim), axis, backward)  24 us
    ppermute x6, starting transfers between devices, padded_2(): lax.ppermute(lax.slice_in_dim(block, 0, width, axis=dim), axis, backward)  20.8 us
    another operation x1, local copies, waits for them, and re-layouts, shards(): return state[None]  20.5 us
    reshape x1, local copies, waits for them, and re-layouts, shards(): state = flat.reshape(nvar, rows, width_y, width_z)  17.8 us
  transfers between devices with their start and end apart: 14, of which 11 were waited for; matrix products, arithmetic and copies ran while one was open for 31% of the time, Pallas kernels for 0%

commit v1 on v0

--- a/solution.py
+++ b/solution.py
@@ -76,7 +76,12 @@
         flat = state.reshape(nvar, total_cells)
         values = flat[:, corner_cell].reshape(nvar, comps, slots, 8, tile)
         packed = jnp.einsum("vcskp,cskp->vcsp", values, held, precision=lax.Precision.HIGHEST)
-        arrived = lax.all_to_all(packed, "comp", split_axis=1, concat_axis=1, tiled=True)
+        arrived = jnp.concatenate(
+            jax.lax.all_to_all(
+                jnp.stack(jnp.split(packed, jax.lax.axis_size("comp"), axis=1)), "comp", 0, 0
+            ),
+            1,
+        )
         incoming = arrived.reshape(nvar, -1)
         flat = flat.at[:, target_cell].set(incoming, mode="drop")
         state = flat.reshape(nvar, rows, width_y, width_z)

time: 570 us -> 579 us (1.016)
  local copies, waits for them, and re-layouts: 381 us -> 390 us
    unnamed x21 -> x51, local copies, waits for them, and re-layouts: 2.41 us -> 11.4 us
where the time goes in v1:
time: 579 us; the launch traced here: 569 us
  local copies, waits for them, and re-layouts  390 us (67%)
  matrix products  59.9 us (10%)
  starting transfers between devices  51.8 us (9%)
  waiting for transfers between devices  37.6 us (6%)
  other arithmetic  15.7 us (3%)
  blocking collectives  13.4 us (2%)
    gather x2, local copies, waits for them, and re-layouts, shards(): values = flat[:, corner_cell].reshape(nvar, comps, slots, 8, tile)  238 us
    scatter x2, local copies, waits for them, and re-layouts, shards(): flat = flat.at[:, target_cell].set(incoming, mode='drop')  64.5 us
    dot_general x18, matrix products, mix(): jnp.einsum('vw,wxyz->vxyz', jac_dim, field, precision=lax.Precision.HIGHEST)  59.9 us
    reshape x2, local copies, waits for them, and re-layouts, shards(): flat = state.reshape(nvar, total_cells)  33.2 us
    ppermute x6, waiting for transfers between devices, padded_2(): lax.ppermute(lax.slice_in_dim(block, 0, width, axis=dim), axis, backward)  24 us
    ppermute x6, starting transfers between devices, padded_2(): lax.ppermute(lax.slice_in_dim(block, 0, width, axis=dim), axis, backward)  20.8 us
    another operation x1, local copies, waits for them, and re-layouts, shards(): return state[None]  20.5 us
    reshape x1, local copies, waits for them, and re-layouts, shards(): state = flat.reshape(nvar, rows, width_y, width_z)  17.8 us
  transfers between devices with their start and end apart: 14, of which 11 were waited for; matrix products, arithmetic and copies ran while one was open for 31% of the time, Pallas kernels for 0%

profile of v1, /device:TPU:27, one launch (start us, length us, event | category | flops | bytes accessed | tf_op | source)
XLA Modules:
  0.0 569.1 jit_solution(6221161298700552198)
XLA Ops:
  0.0 9.3 %all-to-all-start = ((f32[16,2,8,128]{3,2,1,0:T(8,128)}), f32[16,2,8,128]{3,2,1,0:T(8,128)S(1)}, u32[]{:S(2)}, u32[]{:S(2)}) async-start(f32[16,2,8,128]{3,2,1,0:T(8,128)} %bitcast.394), calls=%async_computation | async-start | bytes 262144 | tf_op jit(solution)/shard_map/all_to_all | solution.py:66
  9.3 2.4 copy.325
  12.4 2.8 collective-permute-start.1
  15.2 2.5 collective-permute-start
  18.3 2.6 fusion.73
  21.0 2.0 fusion.76
  23.1 3.7 collective-permute-done
  26.8 7.2 %negate_divide_fusion.1 = (f32[6,8,32,256]{3,0,2,1:T(8,128)S(1)}, f32[6,8,32,256]{3,0,2,1:T(8,128)S(1)}) fusion(f32[8,32,256]{2,1,0:T(8,128)S(1)} %get-tuple-element.18, f32[6,8,32,256]{3,0,2,1:T(8,128)S(1)} %bitcast.341, f32[6,1,32,256]{3,0,2,1:T(8,128)} %collective-permute-done.1, f32[6,1,32,256]{3,0,2,1:T(8,128)} %collective-permute-done, ...), kind=kOutput, calls=%fused_computation.119 | convolution fusion | flops 38141952 | bytes 14683136 | tf_op jit(solution)/shard_map/vw,wxyz->vxyz/dot_general | solution.py:25
  34.1 2.6 fusion.64
  38.6 3.6 collective-permute-start.2
  42.2 2.0 fusion.67
  45.2 4.0 collective-permute-done.2
  49.2 3.9 fusion.18
  53.2 2.6 fusion.53
  57.7 3.9 collective-permute-start.4
  61.6 2.0 fusion.56
  63.7 3.9 collective-permute-done.4
  67.6 4.9 fusion.14
  72.5 16.8 %copy.222 = f32[6,65536]{0,1:T(8,128)} copy(f32[6,65536]{1,0:T(8,128)S(1)} %bitcast.345) | data formatting | bytes 3145728 | tf_op jit(solution)/shard_map/reshape | solution.py:76
  89.3 118.8 %gather_fusion = f32[32768,6]{1,0:T(8,128)} fusion(f32[6,65536]{0,1:T(8,128)} %copy.222, s32[32768]{0:T(1024)S(1)} %broadcast_clamp_fusion), kind=kCustom, calls=%fused_computation | custom fusion | bytes 1703936 | tf_op jit(solution)/shard_map/gather | solution.py:77
  208.1 7.7 %multiply_reduce_fusion.1 = f32[16,2,128,6]{3,2,1,0:T(8,128)S(1)} fusion(f32[16,2,128,8,6]{4,2,3,1,0:T(8,128)} %bitcast.342, f32[16,2,128,8]{2,3,1,0:T(8,128)S(1)} %bitcast.346), kind=kLoop, calls=%fused_computation.5 | loop fusion | flops 368640 | bytes 1015808
  226.0 9.3 %all-to-all-start.1 = ((f32[16,6,1,2,128]{4,3,2,1,0:T(2,128)}), f32[16,6,1,2,128]{4,3,2,1,0:T(2,128)S(1)}, u32[]{:S(2)}, u32[]{:S(2)}) async-start(f32[16,6,1,2,128]{4,3,2,1,0:T(2,128)} %constant_dynamic-update-slice_fusion), calls=%async_computation.1 | async-start | bytes 196608 | tf_op jit(solution)/shard_map/all_to_all | solution.py:80
  235.4 8.4 %all-to-all-done.1 = f32[16,6,1,2,128]{4,3,2,1,0:T(2,128)S(1)} async-done(((f32[16,6,1,2,128]{4,3,2,1,0:T(2,128)}), f32[16,6,1,2,128]{4,3,2,1,0:T(2,128)S(1)}, u32[]{:S(2)}, u32[]{:S(2)}) %all-to-all-start.1) | async-done | bytes 98336 | tf_op jit(solution)/shard_map/all_to_all | solution.py:80
  244.6 32.3 %scatter_fusion = f32[6,65536]{0,1:T(8,128)} fusion(f32[6,65536]{0,1:T(8,128)} %copy.222, s32[4096]{0:T(1024)S(1)} %bitcast.391, f32[4096,6]{1,0:T(8,128)S(1)} %copy.223), kind=kCustom, calls=%fused_computation.2 | custom fusion | bytes 311296 | tf_op jit(solution)/shard_map/scatter | solution.py:86
  276.9 17.8 %copy.232 = f32[6,8,32,256]{3,0,2,1:T(8,128)S(1)} copy(f32[6,8,32,256]{0,3,2,1:T(8,128)} %bitcast.336) | data formatting | bytes 3145728 | tf_op jit(solution)/shard_map/reshape | solution.py:87
  294.7 2.6 fusion.42
  299.3 3.6 collective-permute-start.6
  303.0 2.1 fusion.45
  305.0 2.3 collective-permute-done.7
  307.3 4.3 collective-permute-done.6
  311.6 5.8 %negate_divide_fusion = (f32[6,8,32,256]{3,0,2,1:T(8,128)S(1)}, f32[6,8,32,256]{3,0,2,1:T(8,128)S(1)}) fusion(f32[8,32,256]{2,1,0:T(8,128)S(1)} %get-tuple-element.18, f32[6,8,32,256]{3,0,2,1:T(8,128)S(1)} %copy.232, f32[6,1,32,256]{3,0,2,1:T(8,128)S(1)} %collective-permute-done.7, f32[6,1,32,256]{3,0,2,1:T(8,128)S(1)} %collective-permute-done.6, ...), kind=kOutput, calls=%fused_computation.91 | convolution fusion | flops 38141952 | bytes 16256000 | tf_op jit(solution)/shard_map/vw,wxyz->vxyz/dot_general | solution.py:25
  317.4 2.6 fusion.33
  320.1 1.9 collective-permute-start.9
  322.0 3.6 collective-permute-start.8
  325.6 2.1 fusion.36
  329.1 4.0 collective-permute-done.8
  333.2 4.2 fusion.8
  337.5 2.6 fusion.22
  342.0 3.6 collective-permute-start.10
  345.7 2.1 fusion.25
  348.2 4.0 collective-permute-done.10
  352.3 5.8 %fusion.4 = f32[6,8,32,256]{3,0,2,1:T(8,128)} fusion(f32[6,8,32,256]{3,0,2,1:T(8,128)S(1)} %copy.232, f32[6,8,32,256]{3,0,2,1:T(8,128)S(1)} %get-tuple-element.25, f32[6,8,32,256]{3,0,2,1:T(8,128)S(1)} %fusion.8, f32[8,32,256,6]{2,3,1,0:T(8,128)S(1)} %fusion.22, f32[8,32,256,6]{2,3,1,0:T(8,128)S(1)} %fusion.25, ...), kind=kOutput, calls=%fused_computation.47 | convolution fusion | flops 37355520 | bytes 15993856 | tf_op jit(solution)/shard_map/vw,wxyz->vxyz/dot_general | solution.py:25
  358.1 16.4 %copy.250 = f32[6,65536]{0,1:T(8,128)} copy(f32[6,65536]{1,0:T(8,128)} %bitcast.344) | data formatting | bytes 3145728 | tf_op jit(solution)/shard_map/reshape | solution.py:76
  374.5 118.8 %gather_fusion.1 = f32[32768,6]{1,0:T(8,128)} fusion(f32[6,65536]{0,1:T(8,128)} %copy.250, s32[32768]{0:T(1024)S(1)} %broadcast_clamp_fusion), kind=kCustom, calls=%fused_computation.1 | custom fusion | bytes 1703936 | tf_op jit(solution)/shard_map/gather | solution.py:77
  493.3 7.7 %multiply_reduce_fusion = f32[16,2,128,6]{3,2,1,0:T(8,128)S(1)} fusion(f32[16,2,128,8,6]{4,2,3,1,0:T(8,128)} %bitcast.343, f32[16,2,128,8]{2,3,1,0:T(8,128)S(1)} %bitcast.347), kind=kLoop, calls=%fused_computation.4 | loop fusion | flops 368640 | bytes 1015808
  501.8 13.4 %all_to_all.15 = f32[16,6,1,2,128]{4,3,2,1,0:T(2,128)S(1)} all-to-all(f32[16,6,1,2,128]{4,3,2,1,0:T(2,128)S(1)} %constant_dynamic-update-slice_fusion.16), channel_id=1, replica_groups=mesh['comp'=16,'blk'=16] {'comp'}, dimensions={0} | all-to-all | bytes 196608 | tf_op jit(solution)/shard_map/all_to_all | solution.py:80
  516.0 32.2 %scatter_fusion.1 = f32[6,65536]{0,1:T(8,128)} fusion(f32[6,65536]{0,1:T(8,128)} %copy.250, s32[4096]{0:T(1024)S(1)} %bitcast.392, f32[4096,6]{1,0:T(8,128)S(1)} %copy.251), kind=kCustom, calls=%fused_computation.3 | custom fusion | bytes 311296 | tf_op jit(solution)/shard_map/scatter | solution.py:86
  548.2 20.5 %copy.252 = f32[1,6,8,32,256]{4,3,2,1,0:T(8,128)} copy(f32[1,6,8,32,256]{1,4,3,2,0:T(8,128)} %bitcast.337) | data formatting | bytes 3145728 | tf_op jit(solution)/shard_map/broadcast_in_dim;reshape | solution.py:88
  (85 shorter events, 24.5 us)
Async XLA Ops:
  0.0 17.7 %copy-start = (s32[1,16,16]{2,1,0:T(8,128)S(1)}, s32[1,16,16]{2,1,0:T(8,128)}, u32[]{:S(2)}) copy-start(s32[1,16,16]{2,1,0:T(8,128)} %param.15) | copy-start | bytes 3076
  0.0 208.1 %all-to-all-start = ((f32[16,2,8,128]{3,2,1,0:T(8,128)}), f32[16,2,8,128]{3,2,1,0:T(8,128)S(1)}, u32[]{:S(2)}, u32[]{:S(2)}) async-start(f32[16,2,8,128]{3,2,1,0:T(8,128)} %bitcast.394), calls=%async_computation | async-start | bytes 262144 | tf_op jit(solution)/shard_map/all_to_all | solution.py:66
  9.3 8.8 %copy-start.7 = (f32[1,3,6,6]{3,0,2,1:T(1,128)S(1)}, f32[1,3,6,6]{3,0,2,1:T(1,128)}, u32[]{:S(2)}) copy-start(f32[1,3,6,6]{3,0,2,1:T(1,128)} %param.11) | copy-start | bytes 1300
  9.3 8.8 %copy-start.5 = (s32[1,1,16,2,8,128]{5,4,3,2,1,0:T(8,128)S(1)}, s32[1,1,16,2,8,128]{5,4,3,2,1,0:T(8,128)}, u32[]{:S(2)}) copy-start(s32[1,1,16,2,8,128]{5,4,3,2,1,0:T(8,128)} %param.12) | copy-start | bytes 393220
  12.4 10.7 %collective-permute-start.1 = (f32[6,1,32,256]{3,0,2,1:T(8,128)}, f32[6,1,32,256]{3,0,2,1:T(8,128)}, u32[]{:S(2)}, u32[]{:S(2)}) collective-permute-start(f32[6,1,32,256]{3,0,2,1:T(8,128)} %get-tuple-element.15), channel_id=1, source_target_pairs={{0,1},{1,2},{2,3},{3,4},{4,5},{5,6},{6,7},{7,8},{8,9},{9,10},{10,1... | collective-permute-start | bytes 589832 | tf_op jit(solution)/shard_map/ppermute | solution.py:16
  15.2 11.6 %collective-permute-start = (f32[6,1,32,256]{3,0,2,1:T(8,128)S(1)}, f32[6,1,32,256]{3,0,2,1:T(8,128)}, u32[]{:S(2)}, u32[]{:S(2)}) collective-permute-start(f32[6,1,32,256]{3,0,2,1:T(8,128)S(1)} %get-tuple-element.16), channel_id=1, source_target_pairs={{1,0},{2,1},{3,2},{4,3},{5,4},{6,5},{7,6},{8,7},{9,8},{10,9},{11,1... | collective-permute-start | bytes 589832 | tf_op jit(solution)/shard_map/ppermute | solution.py:19
  21.0 2.1 copy-start.4
  21.0 5.9 %copy-start.8 = (f32[1,6,8,32,256]{4,3,2,1,0:T(8,128)S(1)}, f32[1,6,8,32,256]{4,3,2,1,0:T(8,128)}, u32[]{:S(2)}) copy-start(f32[1,6,8,32,256]{4,3,2,1,0:T(8,128)} %param.9) | copy-start | bytes 4718596
  36.7 8.5 %collective-permute-start.3 = (f32[6,1,32,256]{3,0,2,1:T(8,128)S(1)}, f32[6,1,32,256]{3,0,2,1:T(8,128)S(1)}, u32[]{:S(2)}, u32[]{:S(2)}) collective-permute-start(f32[6,1,32,256]{3,0,2,1:T(8,128)S(1)} %get-tuple-element.13), channel_id=1, source_target_pairs={{0,1},{1,2},{2,3},{3,4},{4,5},{5,6},{6,7},{7,8},{8,9},{9,10},{10,1... | collective-permute-start | bytes 589832 | tf_op jit(solution)/shard_map/ppermute | solution.py:16
  38.6 10.6 %collective-permute-start.2 = (f32[6,1,32,256]{3,0,2,1:T(8,128)S(1)}, f32[6,1,32,256]{3,0,2,1:T(8,128)S(1)}, u32[]{:S(2)}, u32[]{:S(2)}) collective-permute-start(f32[6,1,32,256]{3,0,2,1:T(8,128)S(1)} %get-tuple-element.14), channel_id=1, source_target_pairs={{1,0},{2,1},{3,2},{4,3},{5,4},{6,5},{7,6},{8,7},{9,8},{10,9},{11,1... | collective-permute-start | bytes 589832 | tf_op jit(solution)/shard_map/ppermute | solution.py:19
  55.8 7.9 %collective-permute-start.5 = (f32[6,1,32,256]{3,0,2,1:T(8,128)S(1)}, f32[6,1,32,256]{3,0,2,1:T(8,128)S(1)}, u32[]{:S(2)}, u32[]{:S(2)}) collective-permute-start(f32[6,1,32,256]{3,0,2,1:T(8,128)S(1)} %get-tuple-element.11), channel_id=1, source_target_pairs={{0,1},{1,2},{2,3},{3,4},{4,5},{5,6},{6,7},{7,8},{8,9},{9,10},{10,1... | collective-permute-start | bytes 589832 | tf_op jit(solution)/shard_map/ppermute | solution.py:16
  57.7 9.8 %copy-start.2 = (f32[1,6,8,32,256]{4,3,2,1,0:T(8,128)S(1)}, f32[1,6,8,32,256]{4,3,2,1,0:T(8,128)}, u32[]{:S(2)}) copy-start(f32[1,6,8,32,256]{4,3,2,1,0:T(8,128)} %param.8) | copy-start | bytes 4718596
  57.7 9.8 %collective-permute-start.4 = (f32[6,1,32,256]{3,0,2,1:T(8,128)S(1)}, f32[6,1,32,256]{3,0,2,1:T(8,128)S(1)}, u32[]{:S(2)}, u32[]{:S(2)}) collective-permute-start(f32[6,1,32,256]{3,0,2,1:T(8,128)S(1)} %get-tuple-element.12), channel_id=1, source_target_pairs={{1,0},{2,1},{3,2},{4,3},{5,4},{6,5},{7,6},{8,7},{9,8},{10,9},{11,1... | collective-permute-start | bytes 589832 | tf_op jit(solution)/shard_map/ppermute | solution.py:19
  215.8 19.5 %copy-start.6 = (s32[1,1,16,2,128]{4,3,2,1,0:T(2,128)S(1)}, s32[1,1,16,2,128]{4,3,2,1,0:T(2,128)}, u32[]{:S(2)}) copy-start(s32[1,1,16,2,128]{4,3,2,1,0:T(2,128)} %param.14) | copy-start | bytes 49156
  226.0 17.8 %all-to-all-start.1 = ((f32[16,6,1,2,128]{4,3,2,1,0:T(2,128)}), f32[16,6,1,2,128]{4,3,2,1,0:T(2,128)S(1)}, u32[]{:S(2)}, u32[]{:S(2)}) async-start(f32[16,6,1,2,128]{4,3,2,1,0:T(2,128)} %constant_dynamic-update-slice_fusion), calls=%async_computation.1 | async-start | bytes 196608 | tf_op jit(solution)/shard_map/all_to_all | solution.py:80
  297.4 9.9 %collective-permute-start.7 = (f32[6,1,32,256]{3,0,2,1:T(8,128)S(1)}, f32[6,1,32,256]{3,0,2,1:T(8,128)S(1)}, u32[]{:S(2)}, u32[]{:S(2)}) collective-permute-start(f32[6,1,32,256]{3,0,2,1:T(8,128)S(1)} %get-tuple-element.9), channel_id=1, source_target_pairs={{0,1},{1,2},{2,3},{3,4},{4,5},{5,6},{6,7},{7,8},{8,9},{9,10},{10,1... | collective-permute-start | bytes 589832 | tf_op jit(solution)/shard_map/ppermute | solution.py:16
  299.3 12.3 %copy-start.3 = (f32[1,6,8,32,256]{4,3,2,1,0:T(8,128)S(1)}, f32[1,6,8,32,256]{4,3,2,1,0:T(8,128)}, u32[]{:S(2)}) copy-start(f32[1,6,8,32,256]{4,3,2,1,0:T(8,128)} %param.8) | copy-start | bytes 4718596
  299.3 12.3 %copy-start.9 = (f32[1,6,8,32,256]{4,3,2,1,0:T(8,128)S(1)}, f32[1,6,8,32,256]{4,3,2,1,0:T(8,128)}, u32[]{:S(2)}) copy-start(f32[1,6,8,32,256]{4,3,2,1,0:T(8,128)} %param.9) | copy-start | bytes 4718596
  299.3 12.3 %collective-permute-start.6 = (f32[6,1,32,256]{3,0,2,1:T(8,128)S(1)}, f32[6,1,32,256]{3,0,2,1:T(8,128)S(1)}, u32[]{:S(2)}, u32[]{:S(2)}) collective-permute-start(f32[6,1,32,256]{3,0,2,1:T(8,128)S(1)} %get-tuple-element.10), channel_id=1, source_target_pairs={{1,0},{2,1},{3,2},{4,3},{5,4},{6,5},{7,6},{8,7},{9,8},{10,9},{11,1... | collective-permute-start | bytes 589832 | tf_op jit(solution)/shard_map/ppermute | solution.py:19
  320.1 9.0 %collective-permute-start.9 = (f32[6,1,32,256]{3,0,2,1:T(8,128)S(1)}, f32[6,1,32,256]{3,0,2,1:T(8,128)S(1)}, u32[]{:S(2)}, u32[]{:S(2)}) collective-permute-start(f32[6,1,32,256]{3,0,2,1:T(8,128)S(1)} %get-tuple-element.7), channel_id=1, source_target_pairs={{0,1},{1,2},{2,3},{3,4},{4,5},{5,6},{6,7},{7,8},{8,9},{9,10},{10,1... | collective-permute-start | bytes 589832 | tf_op jit(solution)/shard_map/ppermute | solution.py:16
  322.0 11.2 %collective-permute-start.8 = (f32[6,1,32,256]{3,0,2,1:T(8,128)S(1)}, f32[6,1,32,256]{3,0,2,1:T(8,128)S(1)}, u32[]{:S(2)}, u32[]{:S(2)}) collective-permute-start(f32[6,1,32,256]{3,0,2,1:T(8,128)S(1)} %get-tuple-element.8), channel_id=1, source_target_pairs={{1,0},{2,1},{3,2},{4,3},{5,4},{6,5},{7,6},{8,7},{9,8},{10,9},{11,1... | collective-permute-start | bytes 589832 | tf_op jit(solution)/shard_map/ppermute | solution.py:19
  340.1 8.1 %collective-permute-start.11 = (f32[6,1,32,256]{3,0,2,1:T(8,128)S(1)}, f32[6,1,32,256]{3,0,2,1:T(8,128)S(1)}, u32[]{:S(2)}, u32[]{:S(2)}) collective-permute-start(f32[6,1,32,256]{3,0,2,1:T(8,128)S(1)} %get-tuple-element.5), channel_id=1, source_target_pairs={{0,1},{1,2},{2,3},{3,4},{4,5},{5,6},{6,7},{7,8},{8,9},{9,10},{10,1... | collective-permute-start | bytes 589832 | tf_op jit(solution)/shard_map/ppermute | solution.py:16
  342.0 10.2 %collective-permute-start.10 = (f32[6,1,32,256]{3,0,2,1:T(8,128)S(1)}, f32[6,1,32,256]{3,0,2,1:T(8,128)S(1)}, u32[]{:S(2)}, u32[]{:S(2)}) collective-permute-start(f32[6,1,32,256]{3,0,2,1:T(8,128)S(1)} %get-tuple-element.6), channel_id=1, source_target_pairs={{1,0},{2,1},{3,2},{4,3},{5,4},{6,5},{7,6},{8,7},{9,8},{10,9},{11,1... | collective-permute-start | bytes 589832 | tf_op jit(solution)/shard_map/ppermute | solution.py:19
  548.2 20.5 %copy-start.1 = (s32[1,16,16]{2,1,0:T(8,128)S(1)}, s32[1,16,16]{2,1,0:T(8,128)}, u32[]{:S(2)}) copy-start(s32[1,16,16]{2,1,0:T(8,128)} %param.15) | copy-start | bytes 3076
